TPU v7x, 32 devices: a whole 2x2x4 slice. The times are simulated.
32 devices in a mesh: section: 4 (over z), ep: 8 (over y, x, core).
Axes of the slice: x: 2, y: 2, z: 4, core: 2. Of those that a mesh axis runs over, the one named last changes fastest.
Arguments:
- flight_a: bfloat16 [4, 1024, 3584], P('section', 'ep'), may hold values from -6 to 6
- flight_b: bfloat16 [4, 1024, 3584], P('section', 'ep'), may hold values from -6 to 6
- routes_a: int32 [4, 1, 1024, 1], P('section', None, 'ep'), may hold values from 0 to 1; in each aligned block of 128 rows (0 to 127, 128 to 255, ..., all dimensions but the last counted through in order) at most 72 rows name the same one
- routes_b: int32 [4, 1, 1024, 1], P('section', None, 'ep'), may hold values from 0 to 1; in each aligned block of 128 rows (0 to 127, 128 to 255, ..., all dimensions but the last counted through in order) at most 72 rows name the same one
- scores_a: float32 [4, 1, 1024, 1], P('section', None, 'ep'), may hold values from 0.5 to 1.5
- scores_b: float32 [4, 1, 1024, 1], P('section', None, 'ep'), may hold values from 0.5 to 1.5
- norm_gain: float32 [4, 3584], P('section'), may hold values from 0.1 to 1.9
- w_gate: bfloat16 [4, 3584, 2048], P('section', None, 'ep'), may hold values from -0.09375 to 0.09375
- w_up: bfloat16 [4, 3584, 2048], P('section', None, 'ep'), may hold values from -0.09375 to 0.09375
- w_down: bfloat16 [4, 2048, 3584], P('section', 'ep'), may hold values from -0.1875 to 0.1875
Outputs:
- out_a: bfloat16 [4, 1024, 3584], P('section', 'ep')
- out_b: bfloat16 [4, 1024, 3584], P('section', 'ep')
Inputs may be any that keep to these rules, and one draw needn't show every extreme that they name: `routes_a`: in each block of 128 rows that one device holds for one layer and step, no expert is named more than 72 times, a bound that some block reaches; a row never names one expert twice. `routes_b`: as for routes_a.
All inputs are finite; a program needn't handle non-finite values.
Results may differ from a plain program's by a relative error of at most 0.0054.
Values may be sent and summed in bfloat16 or wider, within the bound.
A program may use at most 128 MiB of HBM per device.

v0:
```python
import jax
import jax.numpy as jnp
from jax import lax
from jax.sharding import PartitionSpec as P

ES = 4
TOPK = 1


EPSILON = 1e-06


def from_behind(value, axis, steps):
    count = lax.axis_size(axis)
    pairs = [(source, (source + steps) % count) for source in range(count)]
    return lax.ppermute(value, axis, pairs)


def rms_norm(current, gain):
    as_float = current.astype(jnp.float32)
    inverse_rms = lax.rsqrt(jnp.mean(as_float * as_float, axis=-1, keepdims=True) + EPSILON)
    return (as_float * inverse_rms * gain).astype(jnp.bfloat16)


def routing(expert_ids, route_weights, expert_count, capacity):
    token_count, top_count = expert_ids.shape
    flat_ids = expert_ids.reshape(token_count * top_count)
    onehot = (flat_ids[:, None] == jnp.arange(expert_count, dtype=jnp.int32)[None, :]).astype(
        jnp.int32
    )
    before = jnp.cumsum(onehot, axis=0) - onehot
    slot_index = jnp.sum(before * onehot, axis=1)
    column = flat_ids * capacity + slot_index
    placed = column[:, None] == jnp.arange(expert_count * capacity, dtype=jnp.int32)[None, :]
    placed = placed.reshape(token_count, top_count, expert_count * capacity)
    picker = jnp.any(placed, axis=1).astype(jnp.bfloat16)
    mixing = jnp.sum(jnp.where(placed, route_weights[:, :, None], 0.0), axis=1)
    return (picker, mixing)


def prepare(current, expert_ids, route_weights, gain, expert_count, capacity):
    normed = rms_norm(current, gain)
    picker, mixing = routing(expert_ids, route_weights, expert_count, capacity)
    feature_width = normed.shape[1]
    slotted = jnp.einsum("ts,td->sd", picker, normed, preferred_element_type=jnp.float32).astype(
        jnp.bfloat16
    )
    slotted = slotted.reshape(expert_count, 1, capacity, feature_width)
    outgoing = jnp.broadcast_to(slotted, (expert_count, ES, capacity, feature_width))
    return (outgoing.reshape(expert_count * ES, capacity, feature_width), mixing)


def expert_pass(outgoing, gate_cols, up_cols, down_part):
    received = lax.all_to_all(outgoing, "ep", split_axis=0, concat_axis=0, tiled=True)
    source_count, slot_count, feature_width = received.shape
    row_block = received.reshape(source_count * slot_count, feature_width)
    gate_act = jnp.dot(row_block, gate_cols, preferred_element_type=jnp.float32)
    up_act = jnp.dot(row_block, up_cols, preferred_element_type=jnp.float32)
    hidden = (jax.nn.silu(gate_act) * up_act).astype(jnp.bfloat16)
    partial_value = jnp.dot(hidden, down_part, preferred_element_type=jnp.float32).astype(
        jnp.bfloat16
    )
    partial_value = partial_value.reshape(source_count, slot_count, feature_width)
    return lax.all_to_all(partial_value, "ep", split_axis=0, concat_axis=0, tiled=True)


def finish(current, returned, mixing, expert_count):
    feature_width = current.shape[1]
    slot_count = returned.shape[1]
    by_slice = returned.astype(jnp.float32).reshape(expert_count, ES, slot_count, feature_width)
    summed = jnp.sum(by_slice, axis=1).reshape(expert_count * slot_count, feature_width)
    moe_out = jnp.dot(
        mixing, summed, precision=lax.Precision.HIGHEST, preferred_element_type=jnp.float32
    )
    return (current.astype(jnp.float32) + moe_out).astype(jnp.bfloat16)


def on_device(
    flight_a, flight_b, routes_a, routes_b, scores_a, scores_b, norm_gain, w_gate, w_up, w_down
):
    ep_count = lax.axis_size("ep")
    expert_count = ep_count // ES
    tok_dev = flight_a.shape[1]
    capacity = min(tok_dev, 9 * tok_dev * TOPK * ES // (8 * ep_count))
    section_index = lax.axis_index("section")
    last_section = lax.axis_size("section") - 1
    gain = norm_gain[0]
    gate_cols = w_gate[0]
    up_cols = w_up[0]
    down_part = w_down[0]
    current_a = flight_a[0]
    current_b = flight_b[0]
    outgoing_a, mixing_a = prepare(
        current_a, routes_a[0, 0], scores_a[0, 0], gain, expert_count, capacity
    )
    outgoing_b, mixing_b = prepare(
        current_b, routes_b[0, 0], scores_b[0, 0], gain, expert_count, capacity
    )
    returned_a = expert_pass(outgoing_a, gate_cols, up_cols, down_part)
    returned_b = expert_pass(outgoing_b, gate_cols, up_cols, down_part)
    updated_a = finish(current_a, returned_a, mixing_a, expert_count)
    updated_b = finish(current_b, returned_b, mixing_b, expert_count)
    current_a = jnp.where(0 <= section_index, updated_a, current_a)
    current_b = jnp.where(section_index + 0 <= last_section, updated_b, current_b)
    current_a = from_behind(current_a, "section", 1)
    current_b = from_behind(current_b, "section", -1)
    return (current_a[None], current_b[None])


def solution(mesh):
    placed = (
        P("section", "ep", None),
        P("section", "ep", None),
        P("section", None, "ep", None),
        P("section", None, "ep", None),
        P("section", None, "ep", None),
        P("section", None, "ep", None),
        P("section", None),
        P("section", None, "ep"),
        P("section", None, "ep"),
        P("section", "ep", None),
    )
    return jax.shard_map(
        on_device,
        mesh=mesh,
        in_specs=placed,
        out_specs=(P("section", "ep", None), P("section", "ep", None)),
        check_vma=False,
    )
```

profile of v0, /device:TPU:0, one launch (start us, length us, event | category | flops | bytes accessed | tf_op | source)
XLA Modules:
  0.0 255.1 jit_solution(12852984667697311953)
XLA Ops:
  0.6 0.0 copy-start
  0.6 0.9 fusion.60
  1.5 0.2 reduce_window_sum.18
  1.7 0.8 select_reduce_fusion
  2.5 0.7 multiply_add_fusion
  3.2 1.4 fusion.5
  4.6 0.8 reduce
  5.4 1.7 convolution_convert_fusion.2
  7.1 2.2 broadcast_in_dim.59
  9.3 0.0 copy-start.3
  9.3 0.0 copy-start.2
  9.3 5.3 %all-to-all-start.2 = ((bf16[8,72,3584]{2,1,0:T(8,128)(2,1)}), bf16[8,72,3584]{2,1,0:T(8,128)(2,1)}, u32[]{:S(2)}, u32[]{:S(2)}) async-start(bf16[8,72,3584]{2,1,0:T(8,128)(2,1)} %bitcast.81), calls=%async_computation.2 | async-start | bytes 8257536 | tf_op jit(solution)/shard_map/all_to_all | solution.py:54
  14.7 0.0 copy-done.3
  14.7 0.1 fusion.61
  14.8 0.2 reduce_window_sum.17
  14.9 0.2 select_reduce_fusion.1
  15.1 0.0 copy-done.2
  15.1 0.3 fusion.4
  15.4 1.6 convolution_convert_fusion.3
  17.0 46.2 %all-to-all-done.2 = bf16[8,72,3584]{2,1,0:T(8,128)(2,1)} async-done(((bf16[8,72,3584]{2,1,0:T(8,128)(2,1)}), bf16[8,72,3584]{2,1,0:T(8,128)(2,1)}, u32[]{:S(2)}, u32[]{:S(2)}) %all-to-all-start.2) | async-done | bytes 4128800 | tf_op jit(solution)/shard_map/all_to_all | solution.py:54
  63.2 3.4 %broadcast_in_dim.54 = bf16[2,4,72,3584]{3,2,1,0:T(8,128)(2,1)} broadcast(bf16[2,72,3584]{2,1,0:T(8,128)(2,1)} %bitcast.85), dimensions={0,2,3} | broadcast | bytes 5160960 | tf_op jit(solution)/shard_map/broadcast_in_dim | solution.py:49
  66.6 4.5 %all-to-all-start = ((bf16[8,72,3584]{2,1,0:T(8,128)(2,1)}), bf16[8,72,3584]{2,1,0:T(8,128)(2,1)}, u32[]{:S(2)}, u32[]{:S(2)}) async-start(bf16[8,72,3584]{2,1,0:T(8,128)(2,1)} %bitcast.82), calls=%async_computation | async-start | bytes 8257536 | tf_op jit(solution)/shard_map/all_to_all | solution.py:54
  71.1 4.0 %fusion.12 = f32[576,256]{1,0:T(8,128)S(1)} fusion(bf16[576,3584]{1,0:T(8,128)(2,1)} %bitcast.24, bf16[1,3584,256]{2,1,0:T(8,128)(2,1)} %param.17), kind=kOutput, calls=%fused_computation.22 | convolution fusion | flops 1056964608 | bytes 6553600 | tf_op jit(solution)/shard_map/dot_general | solution.py:57
  75.1 0.0 copy-done
  75.1 9.1 %convolution_convert_fusion = bf16[576,3584]{1,0:T(8,128)(2,1)} fusion(bf16[1,256,3584]{2,1,0:T(8,128)(2,1)S(1)} %copy-done, bf16[576,3584]{1,0:T(8,128)(2,1)} %bitcast.24, bf16[1,3584,256]{2,1,0:T(8,128)(2,1)} %param.18, f32[576,256]{1,0:T(8,128)S(1)} %fusion.12), kind=kOutput, calls=%fused_computation.2 | convolution fusion | flops 2116878336 | bytes 12517376 | tf_op jit(solution)/shard_map/dot_general | solution.py:60
  84.3 35.3 %all-to-all-done = bf16[8,72,3584]{2,1,0:T(8,128)(2,1)} async-done(((bf16[8,72,3584]{2,1,0:T(8,128)(2,1)}), bf16[8,72,3584]{2,1,0:T(8,128)(2,1)}, u32[]{:S(2)}, u32[]{:S(2)}) %all-to-all-start) | async-done | bytes 4128800 | tf_op jit(solution)/shard_map/all_to_all | solution.py:54
  119.5 4.6 %all-to-all-start.3 = ((bf16[8,72,3584]{2,1,0:T(8,128)(2,1)}), bf16[8,72,3584]{2,1,0:T(8,128)(2,1)}, u32[]{:S(2)}, u32[]{:S(2)}) async-start(bf16[8,72,3584]{2,1,0:T(8,128)(2,1)} %bitcast.88), calls=%async_computation.3 | async-start | bytes 8257536 | tf_op jit(solution)/shard_map/all_to_all | solution.py:64
  124.1 4.0 %fusion.14 = f32[576,256]{1,0:T(8,128)S(1)} fusion(bf16[576,3584]{1,0:T(8,128)(2,1)} %bitcast.8, bf16[1,3584,256]{2,1,0:T(8,128)(2,1)} %param.17), kind=kOutput, calls=%fused_computation.24 | convolution fusion | flops 1056964608 | bytes 6553600 | tf_op jit(solution)/shard_map/dot_general | solution.py:57
  128.1 9.1 %convolution_convert_fusion.1 = bf16[576,3584]{1,0:T(8,128)(2,1)} fusion(bf16[1,256,3584]{2,1,0:T(8,128)(2,1)S(1)} %copy-done, bf16[576,3584]{1,0:T(8,128)(2,1)} %bitcast.8, bf16[1,3584,256]{2,1,0:T(8,128)(2,1)} %param.18, f32[576,256]{1,0:T(8,128)S(1)} %fusion.14), kind=kOutput, calls=%fused_computation.3 | convolution fusion | flops 2116878336 | bytes 12517376 | tf_op jit(solution)/shard_map/dot_general | solution.py:60
  137.2 35.3 %all-to-all-done.3 = bf16[8,72,3584]{2,1,0:T(8,128)(2,1)} async-done(((bf16[8,72,3584]{2,1,0:T(8,128)(2,1)}), bf16[8,72,3584]{2,1,0:T(8,128)(2,1)}, u32[]{:S(2)}, u32[]{:S(2)}) %all-to-all-start.3) | async-done | bytes 4128800 | tf_op jit(solution)/shard_map/all_to_all | solution.py:64
  172.5 4.7 %all-to-all-start.1 = ((bf16[8,72,3584]{2,1,0:T(8,128)(2,1)}), bf16[8,72,3584]{2,1,0:T(8,128)(2,1)}, u32[]{:S(2)}, u32[]{:S(2)}) async-start(bf16[8,72,3584]{2,1,0:T(8,128)(2,1)} %bitcast.87), calls=%async_computation.1 | async-start | bytes 8257536 | tf_op jit(solution)/shard_map/all_to_all | solution.py:64
  177.2 0.0 copy-start.1
  177.2 0.0 copy-start.4
  177.2 3.1 %convert_reduce_fusion = f32[2,72,3584]{2,1,0:T(8,128)S(1)} fusion(bf16[8,72,3584]{2,1,0:T(8,128)(2,1)} %all-to-all-done.3), kind=kLoop, calls=%fused_computation | loop fusion | flops 3612672 | bytes 6193152 | tf_op jit(solution)/shard_map/reduce_sum | solution.py:71
  180.4 0.0 copy-done.1
  180.4 0.0 copy-done.4
  180.4 2.8 %fusion.2 = bf16[128,3584]{1,0:T(8,128)(2,1)} fusion(f32[144,3584]{1,0:T(8,128)S(1)} %bitcast.83, bf16[1,128,3584]{2,1,0:T(8,128)(2,1)S(1)} %copy-done.1, pred[]{:T(512)S(6)} %le.3, f32[128]{0:T(128)S(1)} %bitcast.94, s32[128]{0:T(128)S(1)} %multiply_add_fusion), kind=kOutput, calls=%fused_computation.10 | convolution fusion | flops 794595328 | bytes 3900417 | tf_op jit(solution)/shard_map/dot_general | solution.py:72
  183.2 0.0 copy-start.5
  183.2 4.3 %collective-permute-start.1 = (bf16[128,3584]{1,0:T(8,128)(2,1)}, bf16[128,3584]{1,0:T(8,128)(2,1)}, u32[]{:S(2)}, u32[]{:S(2)}) collective-permute-start(bf16[128,3584]{1,0:T(8,128)(2,1)} %fusion.2), channel_id=1, source_target_pairs={{0,24},{8,0},{16,8},{24,16},{1,25},{9,1},{17,9},{25,17},{2,26},{10... | collective-permute-start | bytes 2752520 | tf_op jit(solution)/shard_map/ppermute | solution.py:16
  187.6 37.9 %all-to-all-done.1 = bf16[8,72,3584]{2,1,0:T(8,128)(2,1)} async-done(((bf16[8,72,3584]{2,1,0:T(8,128)(2,1)}), bf16[8,72,3584]{2,1,0:T(8,128)(2,1)}, u32[]{:S(2)}, u32[]{:S(2)}) %all-to-all-start.1) | async-done | bytes 4128800 | tf_op jit(solution)/shard_map/all_to_all | solution.py:64
  225.4 3.1 %convert_reduce_fusion.1 = f32[2,72,3584]{2,1,0:T(8,128)S(1)} fusion(bf16[8,72,3584]{2,1,0:T(8,128)(2,1)} %all-to-all-done.1), kind=kLoop, calls=%fused_computation.1 | loop fusion | flops 3612672 | bytes 6193152 | tf_op jit(solution)/shard_map/reduce_sum | solution.py:71
  228.5 0.0 copy-done.5
  228.5 1.9 fusion.3
  230.4 2.4 collective-permute-start
  232.8 0.0 collective-permute-done.1
  232.8 19.2 %collective-permute-done = bf16[128,3584]{1,0:T(8,128)(2,1)S(1)} collective-permute-done((bf16[128,3584]{1,0:T(8,128)(2,1)S(1)}, bf16[128,3584]{1,0:T(8,128)(2,1)S(1)}, u32[]{:S(2)}, u32[]{:S(2)}) %collective-permute-start) | collective-permute-done | bytes 917536 | tf_op jit(solution)/shard_map/ppermute | solution.py:16
  252.0 0.9 copy.14
  253.0 2.2 copy.15
  (3 shorter events, 0.0 us)
Async XLA Ops:
  0.6 74.5 %copy-start = (bf16[1,256,3584]{2,1,0:T(8,128)(2,1)S(1)}, bf16[1,256,3584]{2,1,0:T(8,128)(2,1)}, u32[]{:S(2)}) copy-start(bf16[1,256,3584]{2,1,0:T(8,128)(2,1)} %param.19) | copy-start | bytes 5505028
  9.3 5.3 %copy-start.3 = (s32[1,1,128,1]{2,3,1,0:T(1,128)S(1)}, s32[1,1,128,1]{2,3,1,0:T(1,128)}, u32[]{:S(2)}) copy-start(s32[1,1,128,1]{2,3,1,0:T(1,128)} %param.12) | copy-start | bytes 1540
  9.3 5.8 %copy-start.2 = (bf16[1,128,3584]{2,1,0:T(8,128)(2,1)S(1)}, bf16[1,128,3584]{2,1,0:T(8,128)(2,1)}, u32[]{:S(2)}) copy-start(bf16[1,128,3584]{2,1,0:T(8,128)(2,1)} %param.10) | copy-start | bytes 2752516
  9.3 53.8 %all-to-all-start.2 = ((bf16[8,72,3584]{2,1,0:T(8,128)(2,1)}), bf16[8,72,3584]{2,1,0:T(8,128)(2,1)}, u32[]{:S(2)}, u32[]{:S(2)}) async-start(bf16[8,72,3584]{2,1,0:T(8,128)(2,1)} %bitcast.81), calls=%async_computation.2 | async-start | bytes 8257536 | tf_op jit(solution)/shard_map/all_to_all | solution.py:54
  66.6 52.9 %all-to-all-start = ((bf16[8,72,3584]{2,1,0:T(8,128)(2,1)}), bf16[8,72,3584]{2,1,0:T(8,128)(2,1)}, u32[]{:S(2)}, u32[]{:S(2)}) async-start(bf16[8,72,3584]{2,1,0:T(8,128)(2,1)} %bitcast.82), calls=%async_computation | async-start | bytes 8257536 | tf_op jit(solution)/shard_map/all_to_all | solution.py:54
  119.5 53.0 %all-to-all-start.3 = ((bf16[8,72,3584]{2,1,0:T(8,128)(2,1)}), bf16[8,72,3584]{2,1,0:T(8,128)(2,1)}, u32[]{:S(2)}, u32[]{:S(2)}) async-start(bf16[8,72,3584]{2,1,0:T(8,128)(2,1)} %bitcast.88), calls=%async_computation.3 | async-start | bytes 8257536 | tf_op jit(solution)/shard_map/all_to_all | solution.py:64
  172.5 52.9 %all-to-all-start.1 = ((bf16[8,72,3584]{2,1,0:T(8,128)(2,1)}), bf16[8,72,3584]{2,1,0:T(8,128)(2,1)}, u32[]{:S(2)}, u32[]{:S(2)}) async-start(bf16[8,72,3584]{2,1,0:T(8,128)(2,1)} %bitcast.87), calls=%async_computation.1 | async-start | bytes 8257536 | tf_op jit(solution)/shard_map/all_to_all | solution.py:64
  177.2 3.2 %copy-start.1 = (bf16[1,128,3584]{2,1,0:T(8,128)(2,1)S(1)}, bf16[1,128,3584]{2,1,0:T(8,128)(2,1)}, u32[]{:S(2)}) copy-start(bf16[1,128,3584]{2,1,0:T(8,128)(2,1)} %param.11) | copy-start | bytes 2752516
  177.2 3.2 %copy-start.4 = (f32[1,1,128,1]{2,3,1,0:T(1,128)S(1)}, f32[1,1,128,1]{2,3,1,0:T(1,128)}, u32[]{:S(2)}) copy-start(f32[1,1,128,1]{2,3,1,0:T(1,128)} %param.15) | copy-start | bytes 1540
  183.2 45.3 %copy-start.5 = (f32[1,1,128,1]{2,3,1,0:T(1,128)S(1)}, f32[1,1,128,1]{2,3,1,0:T(1,128)}, u32[]{:S(2)}) copy-start(f32[1,1,128,1]{2,3,1,0:T(1,128)} %param.14) | copy-start | bytes 1540
  183.2 49.6 %collective-permute-start.1 = (bf16[128,3584]{1,0:T(8,128)(2,1)}, bf16[128,3584]{1,0:T(8,128)(2,1)}, u32[]{:S(2)}, u32[]{:S(2)}) collective-permute-start(bf16[128,3584]{1,0:T(8,128)(2,1)} %fusion.2), channel_id=1, source_target_pairs={{0,24},{8,0},{16,8},{24,16},{1,25},{9,1},{17,9},{25,17},{2,26},{10... | collective-permute-start | bytes 2752520 | tf_op jit(solution)/shard_map/ppermute | solution.py:16
  230.4 21.6 %collective-permute-start = (bf16[128,3584]{1,0:T(8,128)(2,1)S(1)}, bf16[128,3584]{1,0:T(8,128)(2,1)S(1)}, u32[]{:S(2)}, u32[]{:S(2)}) collective-permute-start(bf16[128,3584]{1,0:T(8,128)(2,1)S(1)} %fusion.3), channel_id=1, source_target_pairs={{0,8},{8,16},{16,24},{24,0},{1,9},{9,17},{17,25},{25,1},{2,10},{10... | collective-permute-start | bytes 2752520 | tf_op jit(solution)/shard_map/ppermute | solution.py:16
where the time goes:
time: 257 us; the launch traced here: 255 us
  waiting for transfers between devices  174 us (68%)
  matrix products  34.2 us (13%)
  starting transfers between devices  25.8 us (10%)
  other arithmetic  11.6 us (5%)
  local copies, waits for them, and re-layouts  8.78 us (3%)
    all_to_all x2, waiting for transfers between devices, expert_pass(): lax.all_to_all(outgoing, 'ep', split_axis=0, concat_axis=0, tiled=True)  81.5 us
    all_to_all x2, waiting for transfers between devices, expert_pass(): lax.all_to_all(partial_value, 'ep', split_axis=0, concat_axis=0, tiled=True)  73.2 us
    ppermute x2, waiting for transfers between devices, from_behind(): return lax.ppermute(value, axis, pairs)  19.2 us
    dot_general x2, matrix products, expert_pass(): jnp.dot(hidden, down_part, preferred_element_type=jnp.float32)  18.2 us
    all_to_all x2, starting transfers between devices, expert_pass(): lax.all_to_all(outgoing, 'ep', split_axis=0, concat_axis=0, tiled=True)  9.87 us
    all_to_all x2, starting transfers between devices, expert_pass(): lax.all_to_all(partial_value, 'ep', split_axis=0, concat_axis=0, tiled=True)  9.27 us
    dot_general x2, matrix products, expert_pass(): gate_act = jnp.dot(row_block, gate_cols, preferred_element_type=jnp.float32)  7.96 us
    ppermute x2, starting transfers between devices, from_behind(): return lax.ppermute(value, axis, pairs)  6.69 us
  transfers between devices with their start and end apart: 6, of which 5 were waited for; matrix products, arithmetic and copies ran while one was open for 15% of the time, Pallas kernels for 0%

commit v1 on v0

v1 whole, which is shorter than its diff:
```python
import functools

import jax
import jax.numpy as jnp
from jax import lax
from jax.experimental import pallas as pl
from jax.experimental.pallas import tpu as pltpu
from jax.sharding import PartitionSpec as P

ES = 4
TOPK = 1
CORES = 2
PAIR = ES // CORES

EPSILON = 1e-06
MESH = pl.DeviceIdType.MESH


def chunk_width(feature_width, most):
    return max(w for w in range(128, most + 1, 128) if feature_width % w == 0)


def window_kernel(
    ep_count,
    section_count,
    fa,
    fb,
    ra,
    rb,
    sa,
    sb,
    gain,
    w_gate,
    w_up,
    w_down,
    out_a,
    out_b,
    wg,
    wu,
    wd,
    own,
    there,
    leave,
    acc_g,
    acc_u,
    hid,
    part_out,
    part_in,
    home_out,
    home_in,
    final,
    w_sem,
    w_send,
    w_recv,
    a_send,
    a_recv,
    b_send,
    b_recv,
    c_send,
    c_recv,
    d_send,
    d_recv,
    e_send,
    e_recv,
    z_send,
    z_recv,
):
    groups = ep_count // ES
    chunks, rows, width = own.shape[1:]
    tok = fa.shape[0]
    both = 2 * tok
    sec = lax.axis_index("section")
    me = lax.axis_index("ep")
    group = me // ES
    pair = (me // CORES) % PAIR
    core = me % CORES

    def at(g, p, c):
        return (sec, g * ES + p * CORES + c)

    def group_at(i):
        return lax.rem(group + i, groups)

    partner = at(group, pair, 1 - core)
    across = at(group, 1 - pair, core)
    after = (lax.rem(sec + 1, section_count), me)
    before_dev = (lax.rem(sec + section_count - 1, section_count), me)

    loads = [
        pltpu.make_async_copy(src.at[0], dst.at[0], w_sem.at[n])
        for n, (src, dst) in enumerate(((w_gate, wg), (w_up, wu), (w_down, wd)))
    ]
    for load in loads:
        load.start()

    barrier = pltpu.get_barrier_semaphore()
    peers = [partner, across, after, before_dev]
    peers += [at(group_at(i), pair, core) for i in range(1, groups)]
    for peer in peers:
        pl.semaphore_signal(barrier, inc=1, device_id=peer, device_id_type=MESH)

    routes = jnp.concatenate([ra[...], rb[...]], axis=1)
    rel = routes - group
    rel = jnp.where(rel < 0, rel + groups, rel)
    padded = -(-groups // 8) * 8
    named = rel == lax.broadcasted_iota(jnp.int32, (padded, both), 0)
    named_f = jnp.where(named, 1.0, 0.0)
    first = lax.broadcasted_iota(jnp.int32, (both, both), 0)
    second = lax.broadcasted_iota(jnp.int32, (both, both), 1)
    earlier = jnp.where(first < second, 1.0, 0.0).astype(jnp.bfloat16)
    count = jnp.dot(named_f.astype(jnp.bfloat16), earlier, preferred_element_type=jnp.float32)
    slot = jnp.sum(count * named_f, axis=0, keepdims=True).astype(jnp.int32)
    place = rel * rows + slot
    diagonal = first == second
    place_col = jnp.sum(
        jnp.where(diagonal, place.astype(jnp.float32), 0.0), axis=1, keepdims=True
    ).astype(jnp.int32)
    scores = jnp.concatenate([sa[...], sb[...]], axis=1)
    score_col = jnp.sum(jnp.where(diagonal, scores, 0.0), axis=1, keepdims=True)
    pickers = [
        jnp.where(
            place == lax.broadcasted_iota(jnp.int32, (rows, both), 0) + i * rows, 1.0, 0.0
        ).astype(jnp.bfloat16)
        for i in range(groups)
    ]
    placers = [
        jnp.where(
            place_col == lax.broadcasted_iota(jnp.int32, (both, rows), 1) + i * rows, 1.0, 0.0
        ).astype(jnp.bfloat16)
        for i in range(groups)
    ]

    def inverse_rms(ref):
        def add(k, total):
            v = ref[:, pl.ds(pl.multiple_of(k * width, 128), width)].astype(jnp.float32)
            return total + jnp.sum(v * v, axis=1, keepdims=True)

        total = lax.fori_loop(0, chunks, add, jnp.zeros((tok, 1), jnp.float32))
        return lax.rsqrt(total / (chunks * width) + EPSILON)

    inv_a = inverse_rms(fa)
    inv_b = inverse_rms(fb)

    acc_g[...] = jnp.zeros_like(acc_g)
    acc_u[...] = jnp.zeros_like(acc_u)

    pl.semaphore_wait(barrier, len(peers))

    def remote(src, dst, send, recv, device):
        return pltpu.make_async_remote_copy(
            src_ref=src,
            dst_ref=dst,
            send_sem=send,
            recv_sem=recv,
            device_id=device,
            device_id_type=MESH,
        )

    def send_weights():
        return [
            remote(src.at[0], dst.at[1], w_send.at[n], w_recv.at[n], partner)
            for n, (src, dst) in enumerate(((w_gate, wg), (w_up, wu), (w_down, wd)))
        ]

    def own_rows(k):
        return remote(own.at[0, k], there.at[0, k], a_send.at[k], a_recv.at[k], across)

    def leaving(i, k):
        return remote(
            leave.at[i - 1, k],
            own.at[groups - i, k],
            b_send.at[i - 1, k],
            b_recv.at[groups - i - 1, k],
            at(group_at(i), pair, core),
        )

    def relay(j, k):
        return remote(
            own.at[j, k], there.at[j, k], c_send.at[j - 1, k], c_recv.at[j - 1, k], across
        )

    def part(j, k):
        return remote(part_out.at[j, k], part_in.at[j, k], d_send.at[j, k], d_recv.at[j, k], across)

    def homeward(j, k):
        return remote(
            home_out.at[j - 1, k],
            home_in.at[groups - j - 1, k],
            e_send.at[j - 1, k],
            e_recv.at[groups - j - 1, k],
            at(group_at(j), pair, core),
        )

    def lanes(k):
        return pl.ds(pl.multiple_of(k * width, 128), width)

    def result_a(k):
        return remote(final.at[0, k], out_a.at[:, lanes(k)], z_send.at[0, k], z_recv.at[0, k], after)

    def result_b(k):
        return remote(
            final.at[1, k], out_b.at[:, lanes(k)], z_send.at[1, k], z_recv.at[1, k], before_dev
        )

    def dispatch(k, _):
        scale = gain[:, lanes(k)]
        na = (fa[:, lanes(k)].astype(jnp.float32) * inv_a * scale).astype(jnp.bfloat16)
        nb = (fb[:, lanes(k)].astype(jnp.float32) * inv_b * scale).astype(jnp.bfloat16)
        normed = jnp.concatenate([na, nb], axis=0)
        for i in range(1, groups):
            leave[i - 1, k] = jnp.dot(
                pickers[i], normed, preferred_element_type=jnp.float32
            ).astype(jnp.bfloat16)
            leaving(i, k).start()
        own[0, k] = jnp.dot(pickers[0], normed, preferred_element_type=jnp.float32).astype(
            jnp.bfloat16
        )
        own_rows(k).start()
        return 0

    lax.fori_loop(0, chunks, dispatch, 0)
    for copy in send_weights():
        copy.start()
    for load in loads:
        load.wait()
    for copy in send_weights():
        copy.wait_recv()

    def project(side, buffer, j, k):
        block = buffer[j, k]
        for half in range(CORES):
            acc_g[side, j, half] += jnp.dot(
                block, wg[half, pl.ds(pl.multiple_of(k * width, 128), width), :],
                preferred_element_type=jnp.float32,
            )
            acc_u[side, j, half] += jnp.dot(
                block, wu[half, pl.ds(pl.multiple_of(k * width, 128), width), :],
                preferred_element_type=jnp.float32,
            )

    def activate(side, j):
        for half in range(CORES):
            g = acc_g[side, j, half]
            hid[side, j, half] = (g / (1.0 + jnp.exp(-g)) * acc_u[side, j, half]).astype(
                jnp.bfloat16
            )

    def down(side, j, k):
        total = jnp.dot(
            hid[side, j, 0], wd[0, :, lanes(k)], preferred_element_type=jnp.float32
        )
        for half in range(1, CORES):
            total += jnp.dot(
                hid[side, j, half], wd[half, :, lanes(k)], preferred_element_type=jnp.float32
            )
        return total

    def arrivals(k, _):
        for j in range(1, groups):
            leaving(groups - j, k).wait_recv()
            relay(j, k).start()
        for j in range(groups):
            project(0, own, j, k)
        return 0

    lax.fori_loop(0, chunks, arrivals, 0)
    for j in range(groups):
        activate(0, j)

    def from_across(k, _):
        own_rows(k).wait_recv()
        project(1, there, 0, k)
        return 0

    lax.fori_loop(0, chunks, from_across, 0)
    activate(1, 0)

    def send_part(j, k):
        part_out[j, k] = down(1, j, k).astype(jnp.bfloat16)
        part(j, k).start()

    send_part(0, 0)

    def from_relay(k, _):
        for j in range(1, groups):
            relay(j, k).wait_recv()
            project(1, there, j, k)
        return 0

    lax.fori_loop(0, chunks, from_relay, 0)
    for j in range(1, groups):
        activate(1, j)

    def send_parts(k, _):
        @pl.when(k > 0)
        def _():
            send_part(0, k)

        for j in range(1, groups):
            send_part(j, k)
        return 0

    lax.fori_loop(0, chunks, send_parts, 0)

    def finish(k):
        part(0, k).wait_recv()
        mine = (down(0, 0, k) + part_in[0, k].astype(jnp.float32)).astype(jnp.bfloat16)
        moe = jnp.dot(placers[0], mine, preferred_element_type=jnp.float32)
        for i in range(1, groups):
            homeward(groups - i, k).wait_recv()
            moe += jnp.dot(placers[i], home_in[i - 1, k], preferred_element_type=jnp.float32)
        moe = moe * score_col
        final[0, k] = (fa[:, lanes(k)].astype(jnp.float32) + moe[:tok]).astype(jnp.bfloat16)
        result_a(k).start()
        final[1, k] = (fb[:, lanes(k)].astype(jnp.float32) + moe[tok:]).astype(jnp.bfloat16)
        result_b(k).start()

    def returns(k, _):
        @pl.when(k < chunks)
        def _():
            for j in range(1, groups):
                part(j, k).wait_recv()
                home_out[j - 1, k] = (down(0, j, k) + part_in[j, k].astype(jnp.float32)).astype(
                    jnp.bfloat16
                )
                homeward(j, k).start()

        @pl.when(k > 0)
        def _():
            finish(k - 1)

        return 0

    lax.fori_loop(0, chunks + 1, returns, 0)

    for copy in send_weights():
        copy.wait_send()

    def drain(k, _):
        own_rows(k).wait_send()
        for i in range(1, groups):
            leaving(i, k).wait_send()
            relay(i, k).wait_send()
            homeward(i, k).wait_send()
        for j in range(groups):
            part(j, k).wait_send()
        result_a(k).wait()
        result_b(k).wait()
        return 0

    lax.fori_loop(0, chunks, drain, 0)


def on_device(
    flight_a, flight_b, routes_a, routes_b, scores_a, scores_b, norm_gain, w_gate, w_up, w_down
):
    ep_count = lax.axis_size("ep")
    section_count = lax.axis_size("section")
    groups = ep_count // ES
    tok, features = flight_a.shape[1:]
    hidden = w_gate.shape[2]
    capacity = min(tok, 9 * tok * TOPK * ES // (8 * ep_count))
    rows = -(-2 * capacity // 16) * 16
    width = chunk_width(features, 512)
    chunks = features // width
    bf16, f32 = jnp.bfloat16, jnp.float32
    others = groups - 1
    dma = pltpu.SemaphoreType.DMA
    vmem = pl.BlockSpec(memory_space=pltpu.VMEM)
    anywhere = pl.BlockSpec(memory_space=pl.ANY)
    out_a, out_b = pl.pallas_call(
        functools.partial(window_kernel, ep_count, section_count),
        out_shape=(
            jax.ShapeDtypeStruct((tok, features), bf16),
            jax.ShapeDtypeStruct((tok, features), bf16),
        ),
        in_specs=[vmem] * 7 + [anywhere] * 3,
        out_specs=(anywhere, anywhere),
        scratch_shapes=[
            pltpu.VMEM((CORES, features, hidden), bf16),
            pltpu.VMEM((CORES, features, hidden), bf16),
            pltpu.VMEM((CORES, hidden, features), bf16),
            pltpu.VMEM((groups, chunks, rows, width), bf16),
            pltpu.VMEM((groups, chunks, rows, width), bf16),
            pltpu.VMEM((others, chunks, rows, width), bf16),
            pltpu.VMEM((PAIR, groups, CORES, rows, hidden), f32),
            pltpu.VMEM((PAIR, groups, CORES, rows, hidden), f32),
            pltpu.VMEM((PAIR, groups, CORES, rows, hidden), bf16),
            pltpu.VMEM((groups, chunks, rows, width), bf16),
            pltpu.VMEM((groups, chunks, rows, width), bf16),
            pltpu.VMEM((others, chunks, rows, width), bf16),
            pltpu.VMEM((others, chunks, rows, width), bf16),
            pltpu.VMEM((2, chunks, tok, width), bf16),
            dma((3,)),
            dma((3,)),
            dma((3,)),
            dma((chunks,)),
            dma((chunks,)),
            dma((others, chunks)),
            dma((others, chunks)),
            dma((others, chunks)),
            dma((others, chunks)),
            dma((groups, chunks)),
            dma((groups, chunks)),
            dma((others, chunks)),
            dma((others, chunks)),
            dma((2, chunks)),
            dma((2, chunks)),
        ],
        compiler_params=pltpu.CompilerParams(
            collective_id=0, has_side_effects=True, vmem_limit_bytes=60 * 1024 * 1024
        ),
    )(
        flight_a[0],
        flight_b[0],
        routes_a.reshape(1, tok),
        routes_b.reshape(1, tok),
        scores_a.reshape(1, tok),
        scores_b.reshape(1, tok),
        norm_gain,
        w_gate,
        w_up,
        w_down,
    )
    return (out_a[None], out_b[None])


def solution(mesh):
    placed = (
        P("section", "ep", None),
        P("section", "ep", None),
        P("section", None, "ep", None),
        P("section", None, "ep", None),
        P("section", None, "ep", None),
        P("section", None, "ep", None),
        P("section", None),
        P("section", None, "ep"),
        P("section", None, "ep"),
        P("section", "ep", None),
    )
    return jax.shard_map(
        on_device,
        mesh=mesh,
        in_specs=placed,
        out_specs=(P("section", "ep", None), P("section", "ep", None)),
        check_vma=False,
    )
```

time: 257 us -> 115 us (0.45)
  waiting for transfers between devices: 174 us -> 0 us
  Pallas kernels: 0 us -> 111 us
  matrix products: 34.2 us -> 0 us
  starting transfers between devices: 25.8 us -> 0 us
  other arithmetic: 11.6 us -> 0 us
  local copies, waits for them, and re-layouts: 8.78 us -> 3.17 us
    all_to_all x4 -> x0, waiting for transfers between devices: 155 us -> none  [the longest x2 81.5 us: expert_pass(): lax.all_to_all(outgoing, 'ep', split_axis=0, concat_axis=0, tiled=True)]
    pallas_call x0 -> x1, Pallas kernels: none -> 111 us  [on_device(): pl.pallas_call(functools.partial(window_kernel, ep_count, section_count),...]
    dot_general x8 -> x0, matrix products: 34.2 us -> none  [the longest x2 18.2 us: expert_pass(): jnp.dot(hidden, down_part, preferred_element_type=jnp.float32)]
    ppermute x2 -> x0, waiting for transfers between devices: 19.2 us -> none  [from_behind(): return lax.ppermute(value, axis, pairs)]
    all_to_all x4 -> x0, starting transfers between devices: 19.1 us -> none  [the longest x2 9.87 us: expert_pass(): lax.all_to_all(outgoing, 'ep', split_axis=0, concat_axis=0, tiled=True)]
    reduce_sum x6 -> x0, other arithmetic: 8.89 us -> none  [the longest x2 6.18 us: finish(): jnp.sum(by_slice, axis=1).reshape(expert_count * slot_count, feature_width)]
    ppermute x2 -> x0, starting transfers between devices: 6.69 us -> none  [from_behind(): return lax.ppermute(value, axis, pairs)]
    broadcast_in_dim x2 -> x0, local copies, waits for them, and re-layouts: 5.67 us -> none  [prepare(): jnp.broadcast_to(slotted, (expert_count, ES, capacity, feature_width))]
  transfers between devices with their start and end apart: 6 -> 0, of which waited for: 5 -> 0; matrix products, arithmetic and copies ran while one was open for 15% -> 0% of each run, Pallas kernels for 0% -> 0%
where the time goes in v1:
time: 115 us
  Pallas kernels  111 us (97%)
  local copies, waits for them, and re-layouts  3.17 us (3%)
    pallas_call x1, Pallas kernels, on_device(): pl.pallas_call(functools.partial(window_kernel, ep_count, section_count),...  111 us
    unnamed x4, local copies, waits for them, and re-layouts  3.17 us

profile of v1, /device:TPU:0, one launch (start us, length us, event | category | flops | bytes accessed | tf_op | source)
XLA Modules:
  0.0 115.1 jit_solution(1226193438609345026)
XLA Ops:
  0.6 111.3 %shard_map.113 = (bf16[128,3584]{1,0:T(8,128)(2,1)}, bf16[128,3584]{1,0:T(8,128)(2,1)}) custom-call(bf16[128,3584]{1,0:T(8,128)(2,1)} %bitcast.8, bf16[128,3584]{1,0:T(8,128)(2,1)} %bitcast.9, s32[1,128]{1,0:T(1,128)} %bitcast.12, s32[1,128]{1,0:T(1,128)} %bitcast.13, f32[1,128]{1,0:T(1,128)} %bitcast.14, f32[1,128]{1,0:T(1,128)} %bitcast.15, ...), custom_call_target="tpu_custom_call" | custom-call | tf_op jit(solution)/shard_map/pallas_call | solution.py:371
  111.9 0.0 copy-start
  111.9 2.2 %copy.14 = bf16[1,128,3584]{2,1,0:T(8,128)(2,1)} copy(bf16[1,128,3584]{2,1,0:T(8,128)(2,1)} %bitcast.11) | data formatting | bytes 1835008
  114.1 0.0 copy-done
  114.1 0.9 copy.15
Async XLA Ops:
  111.9 2.3 %copy-start = (bf16[128,3584]{1,0:T(8,128)(2,1)S(1)}, bf16[128,3584]{1,0:T(8,128)(2,1)}, u32[]{:S(2)}) copy-start(bf16[128,3584]{1,0:T(8,128)(2,1)} %get-tuple-element.5) | copy-start | bytes 2752516

commit v2 on v1

--- a/solution.py
+++ b/solution.py
@@ -69,6 +69,7 @@
     chunks, rows, width = own.shape[1:]
     tok = fa.shape[0]
     both = 2 * tok
+    ahead = min(2, chunks)
     sec = lax.axis_index("section")
     me = lax.axis_index("ep")
     group = me // ES
@@ -279,7 +280,7 @@
         part_out[j, k] = down(1, j, k).astype(jnp.bfloat16)
         part(j, k).start()
 
-    send_part(0, 0)
+    lax.fori_loop(0, ahead, lambda k, _: send_part(0, k) or 0, 0)
 
     def from_relay(k, _):
         for j in range(1, groups):
@@ -292,12 +293,13 @@
         activate(1, j)
 
     def send_parts(k, _):
-        @pl.when(k > 0)
+        for j in range(1, groups):
+            send_part(j, k)
+
+        @pl.when(k >= ahead)
         def _():
             send_part(0, k)
 
-        for j in range(1, groups):
-            send_part(j, k)
         return 0
 
     lax.fori_loop(0, chunks, send_parts, 0)
@@ -361,7 +363,7 @@
     hidden = w_gate.shape[2]
     capacity = min(tok, 9 * tok * TOPK * ES // (8 * ep_count))
     rows = -(-2 * capacity // 16) * 16
-    width = chunk_width(features, 512)
+    width = chunk_width(features, 256)
     chunks = features // width
     bf16, f32 = jnp.bfloat16, jnp.float32
     others = groups - 1
@@ -371,11 +373,11 @@
     out_a, out_b = pl.pallas_call(
         functools.partial(window_kernel, ep_count, section_count),
         out_shape=(
-            jax.ShapeDtypeStruct((tok, features), bf16),
-            jax.ShapeDtypeStruct((tok, features), bf16),
+            pltpu.VMEM((tok, features), bf16),
+            pltpu.VMEM((tok, features), bf16),
         ),
         in_specs=[vmem] * 7 + [anywhere] * 3,
-        out_specs=(anywhere, anywhere),
+        out_specs=(vmem, vmem),
         scratch_shapes=[
             pltpu.VMEM((CORES, features, hidden), bf16),
             pltpu.VMEM((CORES, features, hidden), bf16),

time: 115 us -> 111 us (0.965)
  Pallas kernels: 111 us -> 108 us
  local copies, waits for them, and re-layouts: 3.17 us -> 1.85 us
    pallas_call x1, Pallas kernels: 111 us -> 108 us  [on_device(): pl.pallas_call(functools.partial(window_kernel, ep_count, section_count),...]
    unnamed x4 -> x2, local copies, waits for them, and re-layouts: 3.17 us -> 1.85 us
where the time goes in v2:
time: 111 us
  Pallas kernels  108 us (97%)
  local copies, waits for them, and re-layouts  1.85 us (2%)
    pallas_call x1, Pallas kernels, on_device(): pl.pallas_call(functools.partial(window_kernel, ep_count, section_count),...  108 us

profile of v2, /device:TPU:0, one launch (start us, length us, event | category | flops | bytes accessed | tf_op | source)
XLA Modules:
  0.0 110.8 jit_solution(8006323887330891928)
XLA Ops:
  0.6 108.3 %shard_map.113 = (bf16[128,3584]{1,0:T(8,128)(2,1)S(1)}, bf16[128,3584]{1,0:T(8,128)(2,1)S(1)}) custom-call(bf16[128,3584]{1,0:T(8,128)(2,1)} %bitcast.10, bf16[128,3584]{1,0:T(8,128)(2,1)} %bitcast.11, s32[1,128]{1,0:T(1,128)} %bitcast.12, s32[1,128]{1,0:T(1,128)} %bitcast.13, f32[1,128]{1,0:T(1,128)} %bitcast.14, f32[1,128]{1,0:T(1,128)} %bitcast.15, ...), custom_call_target="tpu_custom_call" | custom-call | tf_op jit(solution)/shard_map/pallas_call | solution.py:373
  109.0 0.9 copy.14
  109.9 0.9 copy.15

commit v3 on v2

--- a/solution.py
+++ b/solution.py
@@ -18,6 +18,15 @@
 
 def chunk_width(feature_width, most):
     return max(w for w in range(128, most + 1, 128) if feature_width % w == 0)
+
+
+def spread_chunks(groups, chunks, rows, both):
+    def longest(n):
+        across = n * both + (chunks - n) * groups * rows
+        between = (groups - 1) * rows * (chunks + n)
+        return max(across, between), n
+
+    return min(longest(n) for n in range(chunks + 1))[1]
 
 
 def window_kernel(
@@ -41,6 +50,11 @@
     own,
     there,
     leave,
+    raw_out,
+    raw_in,
+    passed,
+    place_out,
+    place_in,
     acc_g,
     acc_u,
     hid,
@@ -50,6 +64,8 @@
     home_in,
     final,
     w_sem,
+    p_send,
+    p_recv,
     w_send,
     w_recv,
     a_send,
@@ -70,6 +86,7 @@
     tok = fa.shape[0]
     both = 2 * tok
     ahead = min(2, chunks)
+    spread = spread_chunks(groups, chunks, rows, both)
     sec = lax.axis_index("section")
     me = lax.axis_index("ep")
     group = me // ES
@@ -118,12 +135,17 @@
     ).astype(jnp.int32)
     scores = jnp.concatenate([sa[...], sb[...]], axis=1)
     score_col = jnp.sum(jnp.where(diagonal, scores, 0.0), axis=1, keepdims=True)
-    pickers = [
-        jnp.where(
-            place == lax.broadcasted_iota(jnp.int32, (rows, both), 0) + i * rows, 1.0, 0.0
-        ).astype(jnp.bfloat16)
-        for i in range(groups)
-    ]
+    place_out[...] = place
+
+    def pick(places):
+        return [
+            jnp.where(
+                places == lax.broadcasted_iota(jnp.int32, (rows, both), 0) + i * rows, 1.0, 0.0
+            ).astype(jnp.bfloat16)
+            for i in range(groups)
+        ]
+
+    pickers = pick(place)
     placers = [
         jnp.where(
             place_col == lax.broadcasted_iota(jnp.int32, (both, rows), 1) + i * rows, 1.0, 0.0
@@ -166,6 +188,21 @@
     def own_rows(k):
         return remote(own.at[0, k], there.at[0, k], a_send.at[k], a_recv.at[k], across)
 
+    def places():
+        return remote(place_out, place_in, p_send.at[0], p_recv.at[0], across)
+
+    def raw_rows(k):
+        return remote(raw_out.at[k], raw_in.at[k], a_send.at[k], a_recv.at[k], across)
+
+    def passing(i, k):
+        return remote(
+            passed.at[i - 1, k],
+            there.at[groups - i, k],
+            c_send.at[i - 1, k],
+            c_recv.at[groups - i - 1, k],
+            at(group_at(i), pair, core),
+        )
+
     def leaving(i, k):
         return remote(
             leave.at[i - 1, k],
@@ -208,6 +245,12 @@
         na = (fa[:, lanes(k)].astype(jnp.float32) * inv_a * scale).astype(jnp.bfloat16)
         nb = (fb[:, lanes(k)].astype(jnp.float32) * inv_b * scale).astype(jnp.bfloat16)
         normed = jnp.concatenate([na, nb], axis=0)
+
+        @pl.when(k < spread)
+        def _():
+            raw_out[k] = normed
+            raw_rows(k).start()
+
         for i in range(1, groups):
             leave[i - 1, k] = jnp.dot(
                 pickers[i], normed, preferred_element_type=jnp.float32
@@ -216,14 +259,21 @@
         own[0, k] = jnp.dot(pickers[0], normed, preferred_element_type=jnp.float32).astype(
             jnp.bfloat16
         )
-        own_rows(k).start()
+
+        @pl.when(k >= spread)
+        def _():
+            own_rows(k).start()
+
         return 0
 
+    places().start()
     lax.fori_loop(0, chunks, dispatch, 0)
     for copy in send_weights():
         copy.start()
     for load in loads:
         load.wait()
+    places().wait_recv()
+    pair_pickers = pick(place_in[...])
     for copy in send_weights():
         copy.wait_recv()
 
@@ -257,23 +307,39 @@
         return total
 
     def arrivals(k, _):
+        @pl.when(k < spread)
+        def _():
+            raw_rows(k).wait_recv()
+            normed = raw_in[k]
+            for i in range(1, groups):
+                passed[i - 1, k] = jnp.dot(
+                    pair_pickers[i], normed, preferred_element_type=jnp.float32
+                ).astype(jnp.bfloat16)
+                passing(i, k).start()
+            there[0, k] = jnp.dot(
+                pair_pickers[0], normed, preferred_element_type=jnp.float32
+            ).astype(jnp.bfloat16)
+
         for j in range(1, groups):
             leaving(groups - j, k).wait_recv()
-            relay(j, k).start()
+
+            @pl.when(k >= spread)
+            def _():
+                relay(j, k).start()
+
+        @pl.when(k >= spread)
+        def _():
+            own_rows(k).wait_recv()
+
         for j in range(groups):
             project(0, own, j, k)
+        project(1, there, 0, k)
         return 0
 
     lax.fori_loop(0, chunks, arrivals, 0)
     for j in range(groups):
         activate(0, j)
 
-    def from_across(k, _):
-        own_rows(k).wait_recv()
-        project(1, there, 0, k)
-        return 0
-
-    lax.fori_loop(0, chunks, from_across, 0)
     activate(1, 0)
 
     def send_part(j, k):
@@ -335,14 +401,25 @@
 
     lax.fori_loop(0, chunks + 1, returns, 0)
 
+    places().wait_send()
     for copy in send_weights():
         copy.wait_send()
 
     def drain(k, _):
-        own_rows(k).wait_send()
+        @pl.when(k < spread)
+        def _():
+            raw_rows(k).wait_send()
+            for i in range(1, groups):
+                passing(i, k).wait_send()
+
+        @pl.when(k >= spread)
+        def _():
+            own_rows(k).wait_send()
+            for i in range(1, groups):
+                relay(i, k).wait_send()
+
         for i in range(1, groups):
             leaving(i, k).wait_send()
-            relay(i, k).wait_send()
             homeward(i, k).wait_send()
         for j in range(groups):
             part(j, k).wait_send()
@@ -385,6 +462,11 @@
             pltpu.VMEM((groups, chunks, rows, width), bf16),
             pltpu.VMEM((groups, chunks, rows, width), bf16),
             pltpu.VMEM((others, chunks, rows, width), bf16),
+            pltpu.VMEM((chunks, 2 * tok, width), bf16),
+            pltpu.VMEM((chunks, 2 * tok, width), bf16),
+            pltpu.VMEM((others, chunks, rows, width), bf16),
+            pltpu.VMEM((1, 2 * tok), jnp.int32),
+            pltpu.VMEM((1, 2 * tok), jnp.int32),
             pltpu.VMEM((PAIR, groups, CORES, rows, hidden), f32),
             pltpu.VMEM((PAIR, groups, CORES, rows, hidden), f32),
             pltpu.VMEM((PAIR, groups, CORES, rows, hidden), bf16),
@@ -394,6 +476,8 @@
             pltpu.VMEM((others, chunks, rows, width), bf16),
             pltpu.VMEM((2, chunks, tok, width), bf16),
             dma((3,)),
+            dma((1,)),
+            dma((1,)),
             dma((3,)),
             dma((3,)),
             dma((chunks,)),

time: 111 us -> 107 us (0.964)
  Pallas kernels: 108 us -> 104 us
    pallas_call x1, Pallas kernels: 108 us -> 104 us  [on_device(): pl.pallas_call(functools.partial(window_kernel, ep_count, section_count),...]
where the time goes in v3:
time: 107 us
  Pallas kernels  104 us (97%)
  local copies, waits for them, and re-layouts  1.85 us (2%)
    pallas_call x1, Pallas kernels, on_device(): pl.pallas_call(functools.partial(window_kernel, ep_count, section_count),...  104 us

profile of v3, /device:TPU:0, one launch (start us, length us, event | category | flops | bytes accessed | tf_op | source)
XLA Modules:
  0.0 106.8 jit_solution(15828485803455054357)
XLA Ops:
  0.6 104.3 %shard_map.113 = (bf16[128,3584]{1,0:T(8,128)(2,1)S(1)}, bf16[128,3584]{1,0:T(8,128)(2,1)S(1)}) custom-call(bf16[128,3584]{1,0:T(8,128)(2,1)} %bitcast.10, bf16[128,3584]{1,0:T(8,128)(2,1)} %bitcast.11, s32[1,128]{1,0:T(1,128)} %bitcast.12, s32[1,128]{1,0:T(1,128)} %bitcast.13, f32[1,128]{1,0:T(1,128)} %bitcast.14, f32[1,128]{1,0:T(1,128)} %bitcast.15, ...), custom_call_target="tpu_custom_call" | custom-call | tf_op jit(solution)/shard_map/pallas_call | solution.py:450
  105.0 0.9 copy.14
  105.9 0.9 copy.15

commit v4 on v3

--- a/solution.py
+++ b/solution.py
@@ -23,7 +23,7 @@
 def spread_chunks(groups, chunks, rows, both):
     def longest(n):
         across = n * both + (chunks - n) * groups * rows
-        between = (groups - 1) * rows * (chunks + n)
+        between = (groups - 1) * rows * (chunks + n + 2)
         return max(across, between), n
 
     return min(longest(n) for n in range(chunks + 1))[1]
@@ -32,8 +32,8 @@
 def window_kernel(
     ep_count,
     section_count,
-    fa,
-    fb,
+    fa_whole,
+    fb_whole,
     ra,
     rb,
     sa,
@@ -44,17 +44,18 @@
     w_down,
     out_a,
     out_b,
+    fa,
+    fb,
     wg,
     wu,
     wd,
     own,
     there,
     leave,
-    raw_out,
     raw_in,
     passed,
-    place_out,
-    place_in,
+    info_out,
+    info_in,
     acc_g,
     acc_u,
     hid,
@@ -64,10 +65,13 @@
     home_in,
     final,
     w_sem,
+    f_sem,
     p_send,
     p_recv,
     w_send,
     w_recv,
+    r_send,
+    r_recv,
     a_send,
     a_recv,
     b_send,
@@ -87,6 +91,7 @@
     both = 2 * tok
     ahead = min(2, chunks)
     spread = spread_chunks(groups, chunks, rows, both)
+    early = min(3, spread)
     sec = lax.axis_index("section")
     me = lax.axis_index("ep")
     group = me // ES
@@ -104,18 +109,24 @@
     after = (lax.rem(sec + 1, section_count), me)
     before_dev = (lax.rem(sec + section_count - 1, section_count), me)
 
+    barrier = pltpu.get_barrier_semaphore()
+    peers = [partner, across, after, before_dev]
+    peers += [at(group_at(i), pair, core) for i in range(1, groups)]
+    for peer in peers:
+        pl.semaphore_signal(barrier, inc=1, device_id=peer, device_id_type=MESH)
+
+    flights = [
+        pltpu.make_async_copy(src, dst, f_sem.at[n])
+        for n, (src, dst) in enumerate(((fa_whole, fa), (fb_whole, fb)))
+    ]
+    for load in flights:
+        load.start()
     loads = [
         pltpu.make_async_copy(src.at[0], dst.at[0], w_sem.at[n])
         for n, (src, dst) in enumerate(((w_gate, wg), (w_up, wu), (w_down, wd)))
     ]
     for load in loads:
         load.start()
-
-    barrier = pltpu.get_barrier_semaphore()
-    peers = [partner, across, after, before_dev]
-    peers += [at(group_at(i), pair, core) for i in range(1, groups)]
-    for peer in peers:
-        pl.semaphore_signal(barrier, inc=1, device_id=peer, device_id_type=MESH)
 
     routes = jnp.concatenate([ra[...], rb[...]], axis=1)
     rel = routes - group
@@ -130,13 +141,6 @@
     slot = jnp.sum(count * named_f, axis=0, keepdims=True).astype(jnp.int32)
     place = rel * rows + slot
     diagonal = first == second
-    place_col = jnp.sum(
-        jnp.where(diagonal, place.astype(jnp.float32), 0.0), axis=1, keepdims=True
-    ).astype(jnp.int32)
-    scores = jnp.concatenate([sa[...], sb[...]], axis=1)
-    score_col = jnp.sum(jnp.where(diagonal, scores, 0.0), axis=1, keepdims=True)
-    place_out[...] = place
-
     def pick(places):
         return [
             jnp.where(
@@ -146,27 +150,6 @@
         ]
 
     pickers = pick(place)
-    placers = [
-        jnp.where(
-            place_col == lax.broadcasted_iota(jnp.int32, (both, rows), 1) + i * rows, 1.0, 0.0
-        ).astype(jnp.bfloat16)
-        for i in range(groups)
-    ]
-
-    def inverse_rms(ref):
-        def add(k, total):
-            v = ref[:, pl.ds(pl.multiple_of(k * width, 128), width)].astype(jnp.float32)
-            return total + jnp.sum(v * v, axis=1, keepdims=True)
-
-        total = lax.fori_loop(0, chunks, add, jnp.zeros((tok, 1), jnp.float32))
-        return lax.rsqrt(total / (chunks * width) + EPSILON)
-
-    inv_a = inverse_rms(fa)
-    inv_b = inverse_rms(fb)
-
-    acc_g[...] = jnp.zeros_like(acc_g)
-    acc_u[...] = jnp.zeros_like(acc_u)
-
     pl.semaphore_wait(barrier, len(peers))
 
     def remote(src, dst, send, recv, device):
@@ -188,11 +171,20 @@
     def own_rows(k):
         return remote(own.at[0, k], there.at[0, k], a_send.at[k], a_recv.at[k], across)
 
-    def places():
-        return remote(place_out, place_in, p_send.at[0], p_recv.at[0], across)
+    def info():
+        return remote(info_out, info_in, p_send.at[0], p_recv.at[0], across)
 
     def raw_rows(k):
-        return remote(raw_out.at[k], raw_in.at[k], a_send.at[k], a_recv.at[k], across)
+        return [
+            remote(
+                src.at[:, lanes(k)],
+                raw_in.at[k, pl.ds(n * tok, tok)],
+                r_send.at[n, k],
+                r_recv.at[n, k],
+                across,
+            )
+            for n, src in enumerate((fa_whole, fb_whole))
+        ]
 
     def passing(i, k):
         return remote(
@@ -240,16 +232,45 @@
             final.at[1, k], out_b.at[:, lanes(k)], z_send.at[1, k], z_recv.at[1, k], before_dev
         )
 
+    def send_raw(k, _):
+        for copy in raw_rows(k):
+            copy.start()
+        return 0
+
+    lax.fori_loop(0, early, send_raw, 0)
+    for copy in send_weights():
+        copy.start()
+
+    def inverse_rms(ref):
+        def add(k, total):
+            for n in range(width // 128):
+                v = ref[:, pl.ds(pl.multiple_of(k * width + n * 128, 128), 128)].astype(
+                    jnp.float32
+                )
+                total += v * v
+            return total
+
+        total = lax.fori_loop(0, chunks, add, jnp.zeros((tok, 128), jnp.float32))
+        total = jnp.sum(total, axis=1, keepdims=True)
+        return lax.rsqrt(total / (chunks * width) + EPSILON)
+
+    flights[0].wait()
+    inv_a = inverse_rms(fa)
+    flights[1].wait()
+    inv_b = inverse_rms(fb)
+    inv = jnp.concatenate([inv_a, inv_b], axis=0)
+    info_out[0:1] = place.astype(jnp.float32)
+    info_out[1:2] = jnp.sum(jnp.where(diagonal, inv, 0.0), axis=0, keepdims=True)
+
     def dispatch(k, _):
         scale = gain[:, lanes(k)]
         na = (fa[:, lanes(k)].astype(jnp.float32) * inv_a * scale).astype(jnp.bfloat16)
         nb = (fb[:, lanes(k)].astype(jnp.float32) * inv_b * scale).astype(jnp.bfloat16)
         normed = jnp.concatenate([na, nb], axis=0)
 
-        @pl.when(k < spread)
-        def _():
-            raw_out[k] = normed
-            raw_rows(k).start()
+        @pl.when(k + early < spread)
+        def _():
+            send_raw(k + early, 0)
 
         for i in range(1, groups):
             leave[i - 1, k] = jnp.dot(
@@ -266,14 +287,28 @@
 
         return 0
 
-    places().start()
-    lax.fori_loop(0, chunks, dispatch, 0)
-    for copy in send_weights():
-        copy.start()
+    dispatch(0, 0)
+    info().start()
+    lax.fori_loop(1, chunks, dispatch, 0)
+    acc_g[...] = jnp.zeros_like(acc_g)
+    acc_u[...] = jnp.zeros_like(acc_u)
+    place_col = jnp.sum(
+        jnp.where(diagonal, place.astype(jnp.float32), 0.0), axis=1, keepdims=True
+    ).astype(jnp.int32)
+    scores = jnp.concatenate([sa[...], sb[...]], axis=1)
+    score_col = jnp.sum(jnp.where(diagonal, scores, 0.0), axis=1, keepdims=True)
+    placers = [
+        jnp.where(
+            place_col == lax.broadcasted_iota(jnp.int32, (both, rows), 1) + i * rows, 1.0, 0.0
+        ).astype(jnp.bfloat16)
+        for i in range(groups)
+    ]
+
     for load in loads:
         load.wait()
-    places().wait_recv()
-    pair_pickers = pick(place_in[...])
+    info().wait_recv()
+    pair_pickers = pick(info_in[0:1].astype(jnp.int32))
+    pair_inv = jnp.sum(jnp.where(diagonal, info_in[1:2], 0.0), axis=1, keepdims=True)
     for copy in send_weights():
         copy.wait_recv()
 
@@ -309,8 +344,11 @@
     def arrivals(k, _):
         @pl.when(k < spread)
         def _():
-            raw_rows(k).wait_recv()
-            normed = raw_in[k]
+            for copy in raw_rows(k):
+                copy.wait_recv()
+            normed = (raw_in[k].astype(jnp.float32) * pair_inv * gain[:, lanes(k)]).astype(
+                jnp.bfloat16
+            )
             for i in range(1, groups):
                 passed[i - 1, k] = jnp.dot(
                     pair_pickers[i], normed, preferred_element_type=jnp.float32
@@ -401,14 +439,15 @@
 
     lax.fori_loop(0, chunks + 1, returns, 0)
 
-    places().wait_send()
+    info().wait_send()
     for copy in send_weights():
         copy.wait_send()
 
     def drain(k, _):
         @pl.when(k < spread)
         def _():
-            raw_rows(k).wait_send()
+            for copy in raw_rows(k):
+                copy.wait_send()
             for i in range(1, groups):
                 passing(i, k).wait_send()
 
@@ -453,9 +492,11 @@
             pltpu.VMEM((tok, features), bf16),
             pltpu.VMEM((tok, features), bf16),
         ),
-        in_specs=[vmem] * 7 + [anywhere] * 3,
+        in_specs=[anywhere] * 2 + [vmem] * 5 + [anywhere] * 3,
         out_specs=(vmem, vmem),
         scratch_shapes=[
+            pltpu.VMEM((tok, features), bf16),
+            pltpu.VMEM((tok, features), bf16),
             pltpu.VMEM((CORES, features, hidden), bf16),
             pltpu.VMEM((CORES, features, hidden), bf16),
             pltpu.VMEM((CORES, hidden, features), bf16),
@@ -463,10 +504,9 @@
             pltpu.VMEM((groups, chunks, rows, width), bf16),
             pltpu.VMEM((others, chunks, rows, width), bf16),
             pltpu.VMEM((chunks, 2 * tok, width), bf16),
-            pltpu.VMEM((chunks, 2 * tok, width), bf16),
             pltpu.VMEM((others, chunks, rows, width), bf16),
-            pltpu.VMEM((1, 2 * tok), jnp.int32),
-            pltpu.VMEM((1, 2 * tok), jnp.int32),
+            pltpu.VMEM((2, 2 * tok), f32),
+            pltpu.VMEM((2, 2 * tok), f32),
             pltpu.VMEM((PAIR, groups, CORES, rows, hidden), f32),
             pltpu.VMEM((PAIR, groups, CORES, rows, hidden), f32),
             pltpu.VMEM((PAIR, groups, CORES, rows, hidden), bf16),
@@ -476,10 +516,13 @@
             pltpu.VMEM((others, chunks, rows, width), bf16),
             pltpu.VMEM((2, chunks, tok, width), bf16),
             dma((3,)),
+            dma((2,)),
             dma((1,)),
             dma((1,)),
             dma((3,)),
             dma((3,)),
+            dma((2, chunks)),
+            dma((2, chunks)),
             dma((chunks,)),
             dma((chunks,)),
             dma((others, chunks)),

time: 107 us -> 106 us (level)
    pallas_call x1, Pallas kernels: 104 us -> 103 us  [on_device(): pl.pallas_call(functools.partial(window_kernel, ep_count, section_count),...]
where the time goes in v4:
time: 106 us; the launch traced here: 105 us
  Pallas kernels  103 us (97%)
  local copies, waits for them, and re-layouts  1.85 us (2%)
    pallas_call x1, Pallas kernels, on_device(): pl.pallas_call(functools.partial(window_kernel, ep_count, section_count),...  103 us

profile of v4, /device:TPU:0, one launch (start us, length us, event | category | flops | bytes accessed | tf_op | source)
XLA Modules:
  0.0 105.4 jit_solution(2220972080018784919)
XLA Ops:
  0.6 103.0 %shard_map.113 = (bf16[128,3584]{1,0:T(8,128)(2,1)S(1)}, bf16[128,3584]{1,0:T(8,128)(2,1)S(1)}) custom-call(bf16[128,3584]{1,0:T(8,128)(2,1)} %bitcast.10, bf16[128,3584]{1,0:T(8,128)(2,1)} %bitcast.11, s32[1,128]{1,0:T(1,128)} %bitcast.12, s32[1,128]{1,0:T(1,128)} %bitcast.13, f32[1,128]{1,0:T(1,128)} %bitcast.14, f32[1,128]{1,0:T(1,128)} %bitcast.15, ...), custom_call_target="tpu_custom_call" | custom-call | tf_op jit(solution)/shard_map/pallas_call | solution.py:489
  103.6 0.9 copy.14
  104.5 0.9 copy.15

commit v5 on v4

--- a/solution.py
+++ b/solution.py
@@ -63,6 +63,10 @@
     part_in,
     home_out,
     home_in,
+    cross_out,
+    cross_in,
+    merged_out,
+    merged_in,
     final,
     w_sem,
     f_sem,
@@ -82,6 +86,10 @@
     d_recv,
     e_send,
     e_recv,
+    x_send,
+    x_recv,
+    m_send,
+    m_recv,
     z_send,
     z_recv,
 ):
@@ -89,9 +97,12 @@
     chunks, rows, width = own.shape[1:]
     tok = fa.shape[0]
     both = 2 * tok
-    ahead = min(2, chunks)
     spread = spread_chunks(groups, chunks, rows, both)
     early = min(3, spread)
+    direct = chunks - spread
+    ahead = min(2, direct)
+    lead = min(direct + 1, chunks)
+    lag = 2
     sec = lax.axis_index("section")
     me = lax.axis_index("ep")
     group = me // ES
@@ -224,6 +235,18 @@
     def lanes(k):
         return pl.ds(pl.multiple_of(k * width, 128), width)
 
+    def cross(j, k):
+        return remote(
+            cross_out.at[j - 1, k],
+            cross_in.at[groups - j - 1, k],
+            x_send.at[j - 1, k],
+            x_recv.at[groups - j - 1, k],
+            at(group_at(j), pair, core),
+        )
+
+    def merged(k):
+        return remote(merged_out.at[k], merged_in.at[k], m_send.at[k], m_recv.at[k], across)
+
     def result_a(k):
         return remote(final.at[0, k], out_a.at[:, lanes(k)], z_send.at[0, k], z_recv.at[0, k], after)
 
@@ -297,17 +320,22 @@
     ).astype(jnp.int32)
     scores = jnp.concatenate([sa[...], sb[...]], axis=1)
     score_col = jnp.sum(jnp.where(diagonal, scores, 0.0), axis=1, keepdims=True)
-    placers = [
-        jnp.where(
-            place_col == lax.broadcasted_iota(jnp.int32, (both, rows), 1) + i * rows, 1.0, 0.0
-        ).astype(jnp.bfloat16)
-        for i in range(groups)
-    ]
-
+    def spot(places_col):
+        return [
+            jnp.where(
+                places_col == lax.broadcasted_iota(jnp.int32, (both, rows), 1) + i * rows, 1.0, 0.0
+            ).astype(jnp.bfloat16)
+            for i in range(groups)
+        ]
+
+    placers = spot(place_col)
     for load in loads:
         load.wait()
     info().wait_recv()
     pair_pickers = pick(info_in[0:1].astype(jnp.int32))
+    pair_placers = spot(
+        jnp.sum(jnp.where(diagonal, info_in[0:1], 0.0), axis=1, keepdims=True).astype(jnp.int32)
+    )
     pair_inv = jnp.sum(jnp.where(diagonal, info_in[1:2], 0.0), axis=1, keepdims=True)
     for copy in send_weights():
         copy.wait_recv()
@@ -384,6 +412,17 @@
         part_out[j, k] = down(1, j, k).astype(jnp.bfloat16)
         part(j, k).start()
 
+    def send_home(j, k):
+        home_out[j - 1, k] = down(0, j, k).astype(jnp.bfloat16)
+        homeward(j, k).start()
+
+    def send_cross(j, k):
+        cross_out[j - 1, k] = down(1, j, k).astype(jnp.bfloat16)
+        cross(j, k).start()
+
+    for k in range(direct, lead):
+        for j in range(1, groups):
+            send_home(j, k)
     lax.fori_loop(0, ahead, lambda k, _: send_part(0, k) or 0, 0)
 
     def from_relay(k, _):
@@ -406,23 +445,49 @@
 
         return 0
 
-    lax.fori_loop(0, chunks, send_parts, 0)
-
-    def finish(k):
-        part(0, k).wait_recv()
-        mine = (down(0, 0, k) + part_in[0, k].astype(jnp.float32)).astype(jnp.bfloat16)
-        moe = jnp.dot(placers[0], mine, preferred_element_type=jnp.float32)
+    for k in range(direct, lead):
+        for j in range(1, groups):
+            send_cross(j, k)
+    lax.fori_loop(0, direct, send_parts, 0)
+
+    def finish(k, split):
+        mine = down(0, 0, k)
+        if not split:
+            part(0, k).wait_recv()
+            mine += part_in[0, k].astype(jnp.float32)
+        moe = jnp.dot(placers[0], mine.astype(jnp.bfloat16), preferred_element_type=jnp.float32)
         for i in range(1, groups):
             homeward(groups - i, k).wait_recv()
             moe += jnp.dot(placers[i], home_in[i - 1, k], preferred_element_type=jnp.float32)
+        if split:
+            merged(k).wait_recv()
+            moe += merged_in[k].astype(jnp.float32)
         moe = moe * score_col
         final[0, k] = (fa[:, lanes(k)].astype(jnp.float32) + moe[:tok]).astype(jnp.bfloat16)
         result_a(k).start()
         final[1, k] = (fb[:, lanes(k)].astype(jnp.float32) + moe[tok:]).astype(jnp.bfloat16)
         result_b(k).start()
 
+    def merge(k):
+        total = jnp.dot(
+            pair_placers[0], down(1, 0, k).astype(jnp.bfloat16), preferred_element_type=jnp.float32
+        )
+        for i in range(1, groups):
+            cross(groups - i, k).wait_recv()
+            total += jnp.dot(
+                pair_placers[i], cross_in[i - 1, k], preferred_element_type=jnp.float32
+            )
+        merged_out[k] = total.astype(jnp.bfloat16)
+        merged(k).start()
+
     def returns(k, _):
-        @pl.when(k < chunks)
+        @pl.when(k + lead < chunks)
+        def _():
+            for j in range(1, groups):
+                send_home(j, k + lead)
+                send_cross(j, k + lead)
+
+        @pl.when(k < direct)
         def _():
             for j in range(1, groups):
                 part(j, k).wait_recv()
@@ -431,13 +496,21 @@
                 )
                 homeward(j, k).start()
 
-        @pl.when(k > 0)
-        def _():
-            finish(k - 1)
+        @pl.when((k >= direct) & (k < chunks))
+        def _():
+            merge(k)
+
+        @pl.when((k >= lag) & (k - lag < direct))
+        def _():
+            finish(k - lag, False)
+
+        @pl.when(k - lag >= direct)
+        def _():
+            finish(k - lag, True)
 
         return 0
 
-    lax.fori_loop(0, chunks + 1, returns, 0)
+    lax.fori_loop(0, chunks + lag, returns, 0)
 
     info().wait_send()
     for copy in send_weights():
@@ -460,8 +533,18 @@
         for i in range(1, groups):
             leaving(i, k).wait_send()
             homeward(i, k).wait_send()
-        for j in range(groups):
-            part(j, k).wait_send()
+
+        @pl.when(k < direct)
+        def _():
+            for j in range(groups):
+                part(j, k).wait_send()
+
+        @pl.when(k >= direct)
+        def _():
+            for j in range(1, groups):
+                cross(j, k).wait_send()
+            merged(k).wait_send()
+
         result_a(k).wait()
         result_b(k).wait()
         return 0
@@ -514,6 +597,10 @@
             pltpu.VMEM((groups, chunks, rows, width), bf16),
             pltpu.VMEM((others, chunks, rows, width), bf16),
             pltpu.VMEM((others, chunks, rows, width), bf16),
+            pltpu.VMEM((others, chunks, rows, width), bf16),
+            pltpu.VMEM((others, chunks, rows, width), bf16),
+            pltpu.VMEM((chunks, 2 * tok, width), bf16),
+            pltpu.VMEM((chunks, 2 * tok, width), bf16),
             pltpu.VMEM((2, chunks, tok, width), bf16),
             dma((3,)),
             dma((2,)),
@@ -533,6 +620,10 @@
             dma((groups, chunks)),
             dma((others, chunks)),
             dma((others, chunks)),
+            dma((others, chunks)),
+            dma((others, chunks)),
+            dma((chunks,)),
+            dma((chunks,)),
             dma((2, chunks)),
             dma((2, chunks)),
         ],

time: 106 us -> 112 us (1.057)
  Pallas kernels: 103 us -> 110 us
    pallas_call x1, Pallas kernels: 103 us -> 110 us  [on_device(): pl.pallas_call(functools.partial(window_kernel, ep_count, section_count),...]
where the time goes in v5:
time: 112 us
  Pallas kernels  110 us (98%)
  local copies, waits for them, and re-layouts  1.85 us (2%)
    pallas_call x1, Pallas kernels, on_device(): pl.pallas_call(functools.partial(window_kernel, ep_count, section_count),...  110 us

profile of v5, /device:TPU:0, one launch (start us, length us, event | category | flops | bytes accessed | tf_op | source)
XLA Modules:
  0.0 112.0 jit_solution(14118801700272993576)
XLA Ops:
  0.6 109.5 %shard_map.113 = (bf16[128,3584]{1,0:T(8,128)(2,1)S(1)}, bf16[128,3584]{1,0:T(8,128)(2,1)S(1)}) custom-call(bf16[128,3584]{1,0:T(8,128)(2,1)} %bitcast.10, bf16[128,3584]{1,0:T(8,128)(2,1)} %bitcast.11, s32[1,128]{1,0:T(1,128)} %bitcast.12, s32[1,128]{1,0:T(1,128)} %bitcast.13, f32[1,128]{1,0:T(1,128)} %bitcast.14, f32[1,128]{1,0:T(1,128)} %bitcast.15, ...), custom_call_target="tpu_custom_call" | custom-call | tf_op jit(solution)/shard_map/pallas_call | solution.py:572
  110.2 0.9 copy.14
  111.1 0.9 copy.15
